TPU v7x, 256 devices: a whole 4x4x8 slice. The times are simulated.
256 devices in a mesh: grp: 8 (over y, core), row: 32 (over z, x).
Axes of the slice: x: 4, y: 4, z: 8, core: 2. Of those that a mesh axis runs over, the one named last changes fastest.
Arguments:
- features: bfloat16 [524288, 256], P(('grp', 'row')), may hold values from -6 to 6
- cotangent: bfloat16 [524288, 256], P(('grp', 'row')), may hold values from -6 to 6
- self_weight: bfloat16 [256, 256], replicated, may hold values from -0.375 to 0.375
- neighbor_weight: bfloat16 [256, 256], replicated, may hold values from -0.375 to 0.375
- tile_values: bfloat16 [256, 64, 128, 128], P(('grp', 'row')), may hold values from 0 to 1
- tile_index: int32 [256, 64, 2], P(('grp', 'row')), may hold values from 0 to 15
- hub_adjacency: bfloat16 [524288, 1024], P(('grp', 'row')), may hold values from 0 to 1
- hub_owner: int32 [8, 8], P('grp'), may hold values from 0 to 31
- send_rows: int32 [256, 8, 64], P(('grp', 'row')), may hold values from 0 to 2047
- cut_adjacency: bfloat16 [524288, 512], P(('grp', 'row')), may hold values from 0 to 1
- degrees: int32 [524288], P(('grp', 'row')), may hold values from 1024 to 2047
Outputs:
- hidden: bfloat16 [524288, 256], P(('grp', 'row'))
- grad_features: bfloat16 [524288, 256], P(('grp', 'row'))
- grad_self: float32 [256, 256], replicated
- grad_neighbor: float32 [256, 256], replicated
Inputs may be any that keep to these rules, and one draw needn't show every extreme that they name: `send_rows`: rows may repeat.
All inputs are finite; a program needn't handle non-finite values.
Results may differ from a plain program's by a relative error of at most 0.014.
Values may be sent and summed in bfloat16 or wider, within the bound.
A program may use at most 128 MiB of HBM per device.

v0:
```python
import jax
import jax.numpy as jnp
from jax import lax
from jax.sharding import PartitionSpec as P

TILE = 128
HUB = 128


def spread(value, axis, root):
    mine = lax.axis_index(axis) == root
    return lax.psum(jnp.where(mine, value, jnp.zeros_like(value)), axis)


def on_device(
    features,
    cotangent,
    self_weight,
    neighbor_weight,
    tile_values,
    tile_index,
    hub_adjacency,
    hub_owner,
    send_rows,
    cut_adjacency,
    degrees,
):
    node_count, width = features.shape
    tile_total = node_count // TILE
    group_count = lax.axis_size("grp")
    section_count = hub_owner.shape[1]
    values = tile_values[0]
    index = tile_index[0]
    owners = hub_owner[0]
    blocks = features.reshape(tile_total, TILE, width)
    row_select = (index[:, 0][None, :] == jnp.arange(tile_total)[:, None]).astype(jnp.float32)
    col_select = (index[:, 1][None, :] == jnp.arange(tile_total)[:, None]).astype(jnp.float32)
    picked = blocks[index[:, 1]]
    product = jnp.einsum("lab,lbf->laf", values, picked, preferred_element_type=jnp.float32)
    local_sum = jnp.einsum(
        "nl,laf->naf", row_select, product, precision=lax.Precision.HIGHEST
    ).reshape(node_count, width)
    heads = features[:HUB]
    hub_sum = jnp.zeros((node_count, width), jnp.float32)
    for section in range(section_count):
        panel = spread(heads, "row", owners[section])
        hub_sum = hub_sum + jnp.dot(
            hub_adjacency[:, section * HUB : (section + 1) * HUB],
            panel,
            preferred_element_type=jnp.float32,
        )
    outgoing = features[send_rows[0]]
    arrived = lax.all_to_all(outgoing, "grp", split_axis=0, concat_axis=0, tiled=True)
    cut_sum = jnp.dot(
        cut_adjacency,
        arrived.reshape(group_count * outgoing.shape[1], width),
        preferred_element_type=jnp.float32,
    )
    scaling = lax.rsqrt(degrees.astype(jnp.float32))[:, None]
    aggregated = ((local_sum + hub_sum + cut_sum) * scaling).astype(jnp.bfloat16)
    before = jnp.dot(features, self_weight, preferred_element_type=jnp.float32) + jnp.dot(
        aggregated, neighbor_weight, preferred_element_type=jnp.float32
    )
    activated, pullback = jax.vjp(jax.nn.gelu, before)
    hidden = activated.astype(jnp.bfloat16)
    grad_before = pullback(cotangent.astype(jnp.float32))[0].astype(jnp.bfloat16)
    rows_dims = (((0,), (0,)), ((), ()))
    cols_dims = (((1,), (1,)), ((), ()))
    self_part = lax.dot_general(
        features, grad_before, rows_dims, preferred_element_type=jnp.float32
    )
    neighbor_part = lax.dot_general(
        aggregated, grad_before, rows_dims, preferred_element_type=jnp.float32
    )
    grad_self, grad_neighbor = lax.psum((self_part, neighbor_part), ("grp", "row"))
    grad_aggregate = (
        lax.dot_general(grad_before, neighbor_weight, cols_dims, preferred_element_type=jnp.float32)
        * scaling
    ).astype(jnp.bfloat16)
    grad_total = lax.dot_general(
        grad_before, self_weight, cols_dims, preferred_element_type=jnp.float32
    )
    agg_blocks = grad_aggregate.reshape(tile_total, TILE, width)[index[:, 0]]
    returned = jnp.einsum("lab,laf->lbf", values, agg_blocks, preferred_element_type=jnp.float32)
    grad_total = grad_total + jnp.einsum(
        "nl,lbf->nbf", col_select, returned, precision=lax.Precision.HIGHEST
    ).reshape(node_count, width)
    hub_terms = lax.dot_general(
        hub_adjacency, grad_aggregate, rows_dims, preferred_element_type=jnp.float32
    ).reshape(section_count, HUB, width)
    totals = lax.psum(hub_terms.astype(jnp.bfloat16), "row").astype(jnp.float32)
    owned = (owners == lax.axis_index("row")).astype(jnp.float32)
    hub_grad = jnp.einsum("s,shf->hf", owned, totals, precision=lax.Precision.HIGHEST)
    grad_total = grad_total.at[:HUB].add(hub_grad)
    back_rows = lax.dot_general(
        cut_adjacency, grad_aggregate, rows_dims, preferred_element_type=jnp.float32
    ).astype(jnp.bfloat16)
    back_rows = back_rows.reshape(group_count, -1, width)
    returned_rows = lax.all_to_all(back_rows, "grp", split_axis=0, concat_axis=0, tiled=True)
    scatter_table = (send_rows[0].reshape(-1)[None, :] == jnp.arange(node_count)[:, None]).astype(
        jnp.bfloat16
    )
    grad_total = grad_total + jnp.dot(
        scatter_table, returned_rows.reshape(-1, width), preferred_element_type=jnp.float32
    )
    return (hidden, grad_total.astype(jnp.bfloat16), grad_self, grad_neighbor)


def solution(mesh):
    in_specs = (
        P(("grp", "row"), None),
        P(("grp", "row"), None),
        P(),
        P(),
        P(("grp", "row"), None, None, None),
        P(("grp", "row"), None, None),
        P(("grp", "row"), None),
        P("grp", None),
        P(("grp", "row"), None, None),
        P(("grp", "row"), None),
        P(("grp", "row")),
    )
    out_specs = (P(("grp", "row"), None), P(("grp", "row"), None), P(), P())
    return jax.shard_map(
        on_device, mesh=mesh, in_specs=in_specs, out_specs=out_specs, check_vma=False
    )
```

profile of v0, /device:TPU:8, one launch (start us, length us, event | category | flops | bytes accessed | tf_op | source)
XLA Modules:
  0.0 638.3 jit_solution(11707294678581093016)
XLA Ops:
  7.2 0.0 copy-start
  7.2 0.0 copy-start.1
  7.2 0.8 compare_select_fusion
  8.1 0.1 reshape.124
  8.2 3.6 gather_fusion.1
  11.7 5.5 all-to-all-start
  17.3 0.6 fusion.52
  22.9 0.8 broadcast_select_fusion
  23.7 0.0 all-reduce.10.cloned.1.call-update
  23.7 0.0 all-reduce.8.cloned.1.call-start
  23.8 0.6 eq.97
  24.4 0.6 slice_bitcast_fusion
  25.0 2.8 gather_fusion
  27.8 6.8 %fusion.25 = f32[64,256,128]{2,1,0:T(8,128)} fusion(bf16[64,128,256]{2,1,0:T(8,128)(2,1)} %gather_fusion, bf16[1,64,128,128]{3,2,1,0:T(8,128)(2,1)S(1)} %copy-done), kind=kOutput, calls=%fused_computation.44 | convolution fusion | flops 536870912 | bytes 14680064 | tf_op jit(solution)/shard_map/lab,lbf->laf/dot_general | solution.py:39
  34.6 9.2 %copy.25 = f32[64,256,128]{1,0,2:T(8,128)} copy(f32[64,256,128]{2,1,0:T(8,128)} %fusion.25) | data formatting | bytes 16777216 | tf_op jit(solution)/shard_map/lab,lbf->laf/dot_general | solution.py:39
  43.8 5.2 fusion.2
  48.9 2.6 copy.18
  51.5 2.9 copy.19
  54.4 0.7 convert_rsqrt_fusion
  55.2 1.8 fusion.53
  57.0 117.7 %all-reduce.10.cloned.1.call-done = (bf16[128,256]{1,0:T(8,128)(2,1)}, bf16[128,256]{1,0:T(8,128)(2,1)}, bf16[128,256]{1,0:T(8,128)(2,1)}, bf16[128,256]{1,0:T(8...) async-done(((bf16[128,256]{1,0:T(8,128)(2,1)}, bf16[128,256]{1,0:T(8,128)(2,1)}, ...) | async-done | bytes 524304 | tf_op jit(solution)/shard_map/psum | solution.py:12
  174.6 1.6 fusion.37
  176.2 0.0 copy-start.5
  176.2 1.6 convolution_add_fusion.8
  177.9 0.7 copy-done.5
  178.6 0.5 convolution_add_fusion.7
  179.1 0.4 copy-done.16
  179.4 0.5 convolution_add_fusion.6
  179.9 0.4 copy-done.15
  180.3 0.5 convolution_add_fusion.5
  180.7 0.4 copy-done.14
  181.1 0.5 convolution_add_fusion.4
  181.6 0.4 copy-done.13
  182.0 0.5 convolution_add_fusion.3
  182.4 1.1 copy-done.4
  183.5 1.8 fusion.9
  185.4 3.1 fusion.10
  188.5 3.0 fusion.15
  191.5 1.1 fusion.54
  192.7 1.2 convolution_bitcast_fusion.1
  193.9 2.7 fusion.12
  196.5 1.7 copy.29
  198.2 2.8 gather_fusion.2
  201.0 6.8 %fusion.23 = f32[64,256,128]{2,1,0:T(8,128)} fusion(bf16[64,128,256]{2,1,0:T(8,128)(2,1)} %gather_fusion.2, bf16[1,64,128,128]{3,2,1,0:T(8,128)(2,1)S(1)} %copy-done), kind=kOutput, calls=%fused_computation.42 | convolution fusion | flops 536870912 | bytes 14680064 | tf_op jit(solution)/shard_map/lab,laf->lbf/dot_general | solution.py:84
  207.8 9.2 %copy.27 = f32[64,256,128]{1,0,2:T(8,128)} copy(f32[64,256,128]{2,1,0:T(8,128)} %fusion.23) | data formatting | bytes 16777216 | tf_op jit(solution)/shard_map/lab,laf->lbf/dot_general | solution.py:84
  217.0 5.2 fusion
  222.2 2.6 copy.22
  224.8 0.0 all-reduce.8.cloned.1.call-update
  224.8 0.0 all-reduce.6.cloned.1.call-start
  224.8 3.4 fusion.28
  228.3 0.9 copy.30
  229.2 0.0 all-reduce.6.cloned.1.call-update
  229.2 2.7 fusion.29
  231.9 0.8 copy.23
  232.8 4.8 all-to-all-start.1
  237.6 3.4 convolution_add_fusion
  241.0 233.6 %all-reduce.8.cloned.1.call-done = (f32[256,256]{0,1:T(8,128)}, f32[256,256]{1,0:T(8,128)}) async-done(((f32[256,256]{0,1:T(8,128)}, f32[256,256]{1,0:T(8,128)}), (f32[256,256]{0,1:T(8,128)}, f32[256,256]{1,0:T(8,128)})) %all-reduce.8.cloned.1.call-update) | async-done | bytes 524304 | tf_op jit(solution)/shard_map/psum | solution.py:75
  474.6 1.8 copy.24
  476.4 148.1 %all-reduce.6.cloned.1.call-done = bf16[8,128,256]{1,0,2:T(8,128)(2,1)} async-done(((bf16[8,128,256]{1,0,2:T(8,128)(2,1)}), bf16[8,128,256]{1,0,2:T(8,128)(2,1)}) %all-reduce.6.cloned.1.call-update) | async-done | bytes 524304 | tf_op jit(solution)/shard_map/psum | solution.py:91
  624.6 1.3 fusion.46
  625.9 0.1 copy.28
  626.0 1.6 fusion.39
  627.6 3.4 fusion.11
  631.1 0.7 copy.43
  (46 shorter events, 0.1 us)
Async XLA Ops:
  7.2 20.6 %copy-start = (bf16[1,64,128,128]{3,2,1,0:T(8,128)(2,1)S(1)}, bf16[1,64,128,128]{3,2,1,0:T(8,128)(2,1)}, u32[]{:S(2)}) copy-start(bf16[1,64,128,128]{3,2,1,0:T(8,128)(2,1)} %param.17) | copy-start | bytes 6291460
  7.2 16.6 %copy-start.20 = (s32[1,8,64]{2,1,0:T(8,128)S(1)}, s32[1,8,64]{2,1,0:T(8,128)}, u32[]{:S(2)}) copy-start(s32[1,8,64]{2,1,0:T(8,128)} %param.21) | copy-start | bytes 6148
  7.2 15.7 %copy-start.1 = (bf16[2048,256]{1,0:T(8,128)(2,1)S(1)}, bf16[2048,256]{1,0:T(8,128)(2,1)}, u32[]{:S(2)}) copy-start(bf16[2048,256]{1,0:T(8,128)(2,1)} %param.13) | copy-start | bytes 3145732
  7.2 10.0 %copy-start.19 = (s32[1,8]{1,0:T(1,128)S(1)}, s32[1,8]{1,0:T(1,128)}, u32[]{:S(2)}) copy-start(s32[1,8]{1,0:T(1,128)} %param.20) | copy-start | bytes 100
  7.2 17.2 %copy-start.23 = (s32[1,64,2]{1,2,0:T(2,128)S(1)}, s32[1,64,2]{1,2,0:T(2,128)}, u32[]{:S(2)}) copy-start(s32[1,64,2]{1,2,0:T(2,128)} %param.18) | copy-start | bytes 1540
  11.7 173.6 %all-to-all-start = ((bf16[8,64,256]{2,1,0:T(8,128)(2,1)}), bf16[8,64,256]{2,1,0:T(8,128)(2,1)S(1)}, u32[]{:S(2)}, u32[]{:S(2)}) async-start(bf16[8,64,256]{2,1,0:T(8,128)(2,1)} %bitcast.18), calls=%async_computation | async-start | bytes 524288 | tf_op jit(solution)/shard_map/all_to_all | solution.py:53
  17.2 157.4 %all-reduce.10.cloned.1.call-start = ((), (), s32[]{:S(2)}) async-start(), calls=%async_computation.4 | async-start | bytes 1048576 | tf_op jit(solution)/shard_map/psum | solution.py:12
  23.7 450.9 %all-reduce.8.cloned.1.call-start = ((), (), s32[]{:S(2)}) async-start(), calls=%async_computation.3 | async-start | bytes 1048576 | tf_op jit(solution)/shard_map/psum | solution.py:75
  51.5 3.6 copy-start.8
  174.6 1.6 copy-start.18
  176.2 2.4 copy-start.5
  176.2 2.4 copy-start.17
  178.6 0.8 copy-start.16
  179.4 0.8 copy-start.15
  180.3 0.8 copy-start.14
  181.1 0.8 copy-start.13
  182.0 1.6 copy-start.4
  182.0 1.6 copy-start.12
  185.3 3.2 copy-start.7
  185.4 3.2 copy-start.10
  185.4 3.2 copy-start.24
  191.5 1.1 copy-start.2
  191.5 2.3 copy-start.11
  207.8 9.2 %copy-start.22 = (s32[64]{0:T(128)S(1)}, s32[64]{0:T(128)}, u32[]{:S(2)}) copy-start(s32[64]{0:T(128)} %get-tuple-element.44) | copy-start | bytes 772
  222.2 2.7 copy-start.6
  224.8 399.8 %all-reduce.6.cloned.1.call-start = ((), (), s32[]{:S(2)}) async-start(), calls=%async_computation.2 | async-start | bytes 1048576 | tf_op jit(solution)/shard_map/psum | solution.py:91
  229.2 8.4 %copy-start.3 = (bf16[2048,256]{1,0:T(8,128)(2,1)S(1)}, bf16[2048,256]{1,0:T(8,128)(2,1)}, u32[]{:S(2)}) copy-start(bf16[2048,256]{1,0:T(8,128)(2,1)} %copy-done.2) | copy-start | bytes 3145732
  232.8 394.9 %all-to-all-start.1 = ((bf16[8,64,256]{2,1,0:T(8,128)(2,1)}), bf16[8,64,256]{2,1,0:T(8,128)(2,1)S(1)}, u32[]{:S(2)}, u32[]{:S(2)}) async-start(bf16[8,64,256]{2,1,0:T(8,128)(2,1)} %bitcast.32), calls=%async_computation.1 | async-start | bytes 524288 | tf_op jit(solution)/shard_map/all_to_all | solution.py:99
  237.6 390.0 %copy-start.21 = (s32[512]{0:T(512)S(1)}, s32[512]{0:T(512)}, u32[]{:S(2)}) copy-start(s32[512]{0:T(512)} %eq.97) | copy-start | bytes 6148
  626.0 5.1 copy-start.9
Sparse Core Ops, SparseCore 0:
  23.8 150.7 all-reduce.9
  224.9 249.6 all-reduce.7
  478.4 146.1 all-reduce.5
where the time goes:
time: 640 us; the launch traced here: 638 us
  waiting for transfers between devices  499 us (78%)
  matrix products  58.4 us (9%)
  local copies, waits for them, and re-layouts  46.5 us (7%)
  between operations  19 us (3%)
  starting transfers between devices  10.4 us (2%)
    psum x1, waiting for transfers between devices, on_device(): lax.psum((self_part, neighbor_part), ('grp', 'row'))  234 us
    psum x1, waiting for transfers between devices, on_device(): totals = lax.psum(hub_terms.astype(jnp.bfloat16), 'row').astype(jnp.float32)  148 us
    psum x1, waiting for transfers between devices, spread(): return lax.psum(jnp.where(mine, value, jnp.zeros_like(value)), axis)  118 us
  transfers between devices with their start and end apart: 5, of which 3 were waited for; matrix products, arithmetic and copies ran while one was open for 9% of the time, Pallas kernels for 0%

commit v1 on v0

--- a/solution.py
+++ b/solution.py
@@ -72,7 +72,7 @@
     neighbor_part = lax.dot_general(
         aggregated, grad_before, rows_dims, preferred_element_type=jnp.float32
     )
-    grad_self, grad_neighbor = lax.psum((self_part, neighbor_part), ("grp", "row"))
+    grad_self, grad_neighbor = lax.psum(lax.psum((self_part, neighbor_part), "row"), "grp")
     grad_aggregate = (
         lax.dot_general(grad_before, neighbor_weight, cols_dims, preferred_element_type=jnp.float32)
         * scaling

time: 640 us -> 600 us (0.938)
  waiting for transfers between devices: 499 us -> 454 us
    psum x1 -> x2, waiting for transfers between devices: 234 us -> 205 us  [the longest x1 147 us: on_device(): lax.psum((self_part, neighbor_part), 'row')]
    psum x1, waiting for transfers between devices: 148 us -> 131 us  [on_device(): totals = lax.psum(hub_terms.astype(jnp.bfloat16), 'row').astype(jnp.float32)]
  transfers between devices with their start and end apart: 5 -> 6, of which waited for: 3 -> 4; matrix products, arithmetic and copies ran while one was open for 9% -> 10% of each run, Pallas kernels for 0% -> 0%
where the time goes in v1:
time: 600 us; the launch traced here: 597 us
  waiting for transfers between devices  454 us (76%)
  matrix products  58.4 us (10%)
  local copies, waits for them, and re-layouts  50.2 us (8%)
  between operations  19.1 us (3%)
  starting transfers between devices  10.4 us (2%)
    psum x1, waiting for transfers between devices, on_device(): lax.psum((self_part, neighbor_part), 'row')  147 us
    psum x1, waiting for transfers between devices, on_device(): totals = lax.psum(hub_terms.astype(jnp.bfloat16), 'row').astype(jnp.float32)  131 us
    psum x1, waiting for transfers between devices, spread(): return lax.psum(jnp.where(mine, value, jnp.zeros_like(value)), axis)  118 us
    psum x1, waiting for transfers between devices, on_device(): lax.psum(lax.psum((self_part, neighbor_part), 'row'), 'grp')  58.2 us
  transfers between devices with their start and end apart: 6, of which 4 were waited for; matrix products, arithmetic and copies ran while one was open for 10% of the time, Pallas kernels for 0%

profile of v1, /device:TPU:8, one launch (start us, length us, event | category | flops | bytes accessed | tf_op | source)
XLA Modules:
  0.0 597.0 jit_solution(7922504569740643192)
XLA Ops:
  7.2 0.8 compare_select_fusion
  8.1 0.1 reshape.124
  8.2 3.6 gather_fusion.1
  11.7 5.5 all-to-all-start
  17.3 0.6 fusion.52
  23.0 0.8 broadcast_select_fusion
  23.8 0.0 all-reduce.14.cloned.1.call-update
  23.8 0.0 all-reduce.8.cloned.1.call-start
  23.8 0.7 eq.97
  24.5 0.6 slice_bitcast_fusion
  25.1 2.8 gather_fusion
  27.9 6.8 %fusion.25 = f32[64,256,128]{2,1,0:T(8,128)} fusion(bf16[64,128,256]{2,1,0:T(8,128)(2,1)} %gather_fusion, bf16[1,64,128,128]{3,2,1,0:T(8,128)(2,1)S(1)} %copy-done), kind=kOutput, calls=%fused_computation.44 | convolution fusion | flops 536870912 | bytes 14680064 | tf_op jit(solution)/shard_map/lab,lbf->laf/dot_general | solution.py:39
  34.7 9.2 %copy.25 = f32[64,256,128]{1,0,2:T(8,128)} copy(f32[64,256,128]{2,1,0:T(8,128)} %fusion.25) | data formatting | bytes 16777216 | tf_op jit(solution)/shard_map/lab,lbf->laf/dot_general | solution.py:39
  43.9 5.2 fusion.2
  49.0 2.6 copy.18
  51.6 2.9 copy.19
  54.6 0.7 convert_rsqrt_fusion
  55.3 1.8 fusion.53
  57.1 117.7 %all-reduce.14.cloned.1.call-done = (bf16[128,256]{1,0:T(8,128)(2,1)}, bf16[128,256]{1,0:T(8,128)(2,1)}, bf16[128,256]{1,0:T(8,128)(2,1)}, bf16[128,256]{1,0:T(8...) async-done(((bf16[128,256]{1,0:T(8,128)(2,1)}, bf16[128,256]{1,0:T(8,128)(2,1)}, ...) | async-done | bytes 524304 | tf_op jit(solution)/shard_map/psum | solution.py:12
  174.7 1.6 fusion.37
  176.3 1.6 convolution_add_fusion.8
  178.0 0.7 copy-done.5
  178.7 0.5 convolution_add_fusion.7
  179.2 0.4 copy-done.17
  179.5 0.5 convolution_add_fusion.6
  180.0 0.4 copy-done.16
  180.4 0.5 convolution_add_fusion.5
  180.8 0.4 copy-done.15
  181.2 0.5 convolution_add_fusion.4
  181.7 0.4 copy-done.14
  182.0 0.5 convolution_add_fusion.3
  182.5 1.1 copy-done.4
  183.6 1.8 fusion.9
  185.5 3.1 fusion.10
  188.7 3.0 fusion.15
  191.7 1.0 copy-done.2
  192.6 1.4 fusion.12
  194.1 2.3 copy.29
  196.4 4.7 fusion.28
  201.1 0.7 fusion.29
  201.8 4.1 gather_fusion.2
  205.8 6.8 %fusion.23 = f32[64,256,128]{2,1,0:T(8,128)} fusion(bf16[64,128,256]{2,1,0:T(8,128)(2,1)} %gather_fusion.2, bf16[1,64,128,128]{3,2,1,0:T(8,128)(2,1)S(1)} %copy-done), kind=kOutput, calls=%fused_computation.42 | convolution fusion | flops 536870912 | bytes 14680064 | tf_op jit(solution)/shard_map/lab,laf->lbf/dot_general | solution.py:84
  212.6 9.2 %copy.27 = f32[64,256,128]{1,0,2:T(8,128)} copy(f32[64,256,128]{2,1,0:T(8,128)} %fusion.23) | data formatting | bytes 16777216 | tf_op jit(solution)/shard_map/lab,laf->lbf/dot_general | solution.py:84
  221.8 5.2 fusion
  227.0 2.6 copy.22
  229.6 0.9 copy.30
  230.5 0.0 all-reduce.8.cloned.1.call-update
  230.5 0.8 copy.23
  231.3 4.8 all-to-all-start.1
  236.1 2.8 fusion.54
  238.9 1.2 convolution_bitcast_fusion.1
  240.1 0.0 all-reduce.10.cloned.1.call-update
  240.1 0.0 all-reduce.12.cloned.1.call-start
  240.2 3.7 convolution_add_fusion
  243.9 131.4 %all-reduce.8.cloned.1.call-done = bf16[8,128,256]{1,0,2:T(8,128)(2,1)} async-done(((bf16[8,128,256]{1,0,2:T(8,128)(2,1)}), bf16[8,128,256]{1,0,2:T(8,128)(2,1)}) %all-reduce.8.cloned.1.call-update) | async-done | bytes 524304 | tf_op jit(solution)/shard_map/psum | solution.py:91
  375.3 1.3 fusion.46
  376.6 0.1 copy.28
  376.7 147.1 %all-reduce.10.cloned.1.call-done = (f32[256,256]{0,1:T(8,128)}, f32[256,256]{1,0:T(8,128)}) async-done(((f32[256,256]{0,1:T(8,128)}, f32[256,256]{1,0:T(8,128)}), (f32[256,256]{0,1:T(8,128)}, f32[256,256]{1,0:T(8,128)})) %all-reduce.10.cloned.1.call-update) | async-done | bytes 524304 | tf_op jit(solution)/shard_map/psum | solution.py:75
  523.8 0.0 all-reduce.12.cloned.1.call-update
  523.8 1.6 fusion.39
  525.4 3.4 fusion.11
  528.8 58.2 %all-reduce.12.cloned.1.call-done = (f32[256,256]{0,1:T(8,128)}, f32[256,256]{1,0:T(8,128)}) async-done(((f32[256,256]{0,1:T(8,128)}, f32[256,256]{1,0:T(8,128)}), (f32[256,256]{0,1:T(8,128)}, f32[256,256]{1,0:T(8,128)})) %all-reduce.12.cloned.1.call-update) | async-done | bytes 524304 | tf_op jit(solution)/shard_map/psum | solution.py:75
  587.0 1.8 copy.24
  588.8 1.7 copy.45
  (51 shorter events, 0.1 us)
Async XLA Ops:
  7.2 20.7 %copy-start = (bf16[1,64,128,128]{3,2,1,0:T(8,128)(2,1)S(1)}, bf16[1,64,128,128]{3,2,1,0:T(8,128)(2,1)}, u32[]{:S(2)}) copy-start(bf16[1,64,128,128]{3,2,1,0:T(8,128)(2,1)} %param.17) | copy-start | bytes 6291460
  7.2 16.7 %copy-start.21 = (s32[1,8,64]{2,1,0:T(8,128)S(1)}, s32[1,8,64]{2,1,0:T(8,128)}, u32[]{:S(2)}) copy-start(s32[1,8,64]{2,1,0:T(8,128)} %param.21) | copy-start | bytes 6148
  7.2 15.8 %copy-start.1 = (bf16[2048,256]{1,0:T(8,128)(2,1)S(1)}, bf16[2048,256]{1,0:T(8,128)(2,1)}, u32[]{:S(2)}) copy-start(bf16[2048,256]{1,0:T(8,128)(2,1)} %param.13) | copy-start | bytes 3145732
  7.2 10.0 %copy-start.20 = (s32[1,8]{1,0:T(1,128)S(1)}, s32[1,8]{1,0:T(1,128)}, u32[]{:S(2)}) copy-start(s32[1,8]{1,0:T(1,128)} %param.20) | copy-start | bytes 100
  7.2 17.3 %copy-start.24 = (s32[1,64,2]{1,2,0:T(2,128)S(1)}, s32[1,64,2]{1,2,0:T(2,128)}, u32[]{:S(2)}) copy-start(s32[1,64,2]{1,2,0:T(2,128)} %param.18) | copy-start | bytes 1540
  11.7 173.7 %all-to-all-start = ((bf16[8,64,256]{2,1,0:T(8,128)(2,1)}), bf16[8,64,256]{2,1,0:T(8,128)(2,1)S(1)}, u32[]{:S(2)}, u32[]{:S(2)}) async-start(bf16[8,64,256]{2,1,0:T(8,128)(2,1)} %bitcast.18), calls=%async_computation | async-start | bytes 524288 | tf_op jit(solution)/shard_map/all_to_all | solution.py:53
  17.2 157.5 %all-reduce.14.cloned.1.call-start = ((), (), s32[]{:S(2)}) async-start(), calls=%async_computation.5 | async-start | bytes 1048576 | tf_op jit(solution)/shard_map/psum | solution.py:12
  23.8 351.5 %all-reduce.8.cloned.1.call-start = ((), (), s32[]{:S(2)}) async-start(), calls=%async_computation.2 | async-start | bytes 1048576 | tf_op jit(solution)/shard_map/psum | solution.py:91
  51.6 3.7 copy-start.11
  174.7 1.6 copy-start.19
  176.3 2.4 copy-start.5
  176.3 2.4 copy-start.18
  178.7 0.8 copy-start.17
  179.5 0.8 copy-start.16
  180.4 0.8 copy-start.15
  181.2 0.8 copy-start.14
  182.0 1.6 copy-start.4
  182.0 1.6 copy-start.13
  185.5 3.2 copy-start.9
  185.5 3.2 copy-start.12
  185.5 3.2 copy-start.25
  188.6 3.0 copy-start.7
  191.7 1.0 copy-start.2
  196.4 4.7 copy-start.6
  196.4 4.7 copy-start.8
  212.6 9.2 %copy-start.23 = (s32[64]{0:T(128)S(1)}, s32[64]{0:T(128)}, u32[]{:S(2)}) copy-start(s32[64]{0:T(128)} %get-tuple-element.46) | copy-start | bytes 772
  227.0 2.6 copy-start.10
  231.3 294.1 %all-to-all-start.1 = ((bf16[8,64,256]{2,1,0:T(8,128)(2,1)}), bf16[8,64,256]{2,1,0:T(8,128)(2,1)S(1)}, u32[]{:S(2)}, u32[]{:S(2)}) async-start(bf16[8,64,256]{2,1,0:T(8,128)(2,1)} %bitcast.32), calls=%async_computation.1 | async-start | bytes 524288 | tf_op jit(solution)/shard_map/all_to_all | solution.py:99
  236.1 287.7 %all-reduce.10.cloned.1.call-start = ((), (), s32[]{:S(2)}) async-start(), calls=%async_computation.3 | async-start | bytes 1048576 | tf_op jit(solution)/shard_map/psum | solution.py:75
  236.1 2.8 copy-start.3
  240.1 346.9 %all-reduce.12.cloned.1.call-start = ((), (), s32[]{:S(2)}) async-start(), calls=%async_computation.4 | async-start | bytes 1048576 | tf_op jit(solution)/shard_map/psum | solution.py:75
  240.2 285.2 %copy-start.22 = (s32[512]{0:T(512)S(1)}, s32[512]{0:T(512)}, u32[]{:S(2)}) copy-start(s32[512]{0:T(512)} %eq.97) | copy-start | bytes 6148
Sparse Core Ops, SparseCore 0:
  23.9 150.7 all-reduce.13
  230.6 144.6 all-reduce.7
  379.3 144.4 all-reduce.9
  526.2 60.7 all-reduce.11
